TPU v7x, 32 devices: a whole 2x2x4 slice. The times are simulated.
32 devices in a mesh: rows: 8 (over z, y), cols: 4 (over x, core).
Axes of the slice: x: 2, y: 2, z: 4, core: 2. Of those that a mesh axis runs over, the one named last changes fastest.
Arguments:
- vectors: float32 [16384, 512], P('rows', 'cols'), may hold values from -6 to 6
- reflectors: float32 [3, 128, 256, 128], P(None, ('rows', 'cols')), may hold values from -1.05 to 1.05, as said below
- factors: float32 [3, 128, 128, 128], P(None, ('rows', 'cols')), may hold values from -0.25 to 1.1, as said below
- starts: int32 [3, 128], P(None, 'rows'), may hold values from 0 to 16256, as said below
Outputs:
- transformed: float32 [16384, 512], P('rows', 'cols')
Inputs may be any that keep to these rules, and one draw needn't show every extreme that they name: `reflectors`: each diamond's matrix is unit lower trapezoidal: entry (i, j) is 1 for i = j and 0 for i < j. `factors`: upper triangular; F is the compact-WY factor of the diamond's reflectors, the inverse of the upper triangle of V^T V with its diagonal halved, so that I - V F V^T is orthogonal. starts[t, g] lies between 128 * g and 128 * g + 64; for the first diamond and for the last diamond of every aligned block of 16 diamonds it equals 128 * g.
All inputs are finite; a program needn't handle non-finite values.
Results may differ from a plain program's by a relative error of at most 0.0003.
Values sent between devices are 32-bit elements; how exact they have to be, the bound alone decides.
A program may use at most 64 MiB of HBM per device.

v0:
```python
import functools

import jax
import jax.numpy as jnp
from jax import lax
from jax.experimental import pallas as pl
from jax.experimental.pallas import tpu as pltpu
from jax.sharding import PartitionSpec as P

MESH = pl.DeviceIdType.MESH
SHIFT = 64
CHUNKS = 4
f32, bf16 = jnp.float32, jnp.bfloat16


def split(x):
    high = x.astype(bf16)
    return high, (x - high.astype(f32)).astype(bf16)


def dot(a, b):
    return jnp.dot(a, b, preferred_element_type=f32)


def product(a, b):
    ah, al = split(a)
    bh, bl = split(b)
    return dot(ah, bh) + (dot(al, bh) + dot(ah, bl))


def kernel(
    n_rows, n_cols,
    vec_ref, pack_ref, start_ref, out_ref,
    gat, work, vhi, vlo, wcat, inflow, head, outb, tailb,
    vec_sem, own_sem, g_send, g_recv, p_send, p_recv, f_send, f_recv,
    i_send, i_recv, h_send, h_recv,
):
    row = lax.axis_index("rows")
    col = lax.axis_index("cols")
    ticks, per, height, block = pack_ref.shape
    rows_here, width = vec_ref.shape
    n_dia = per * n_cols
    reach = height + SHIFT
    chunk = width // CHUNKS
    chips = n_cols // 2
    chip, core = lax.div(col, 2), lax.rem(col, 2)
    partner = chip * 2 + 1 - core
    above, below = lax.rem(row + n_rows - 1, n_rows), lax.rem(row + 1, n_rows)

    def peer_of(j):
        return lax.rem(chip + j, chips) * 2 + core

    def share(tick, owner):
        return gat.at[tick, pl.ds(owner * per, per)]

    vec_copy = pltpu.make_async_copy(
        vec_ref, work.at[pl.ds(0, rows_here), pl.ds(0, width)], vec_sem)
    vec_copy.start()

    def own_copy(tick):
        return pltpu.make_async_copy(pack_ref.at[tick], share(tick, col), own_sem.at[tick])

    barrier = pltpu.get_barrier_semaphore()
    for there in (above, below):
        pl.semaphore_signal(barrier, inc=1, device_id={"rows": there}, device_id_type=MESH)
    for j in range(1, chips):
        pl.semaphore_signal(barrier, inc=1, device_id={"cols": peer_of(j)}, device_id_type=MESH)
    pl.semaphore_signal(barrier, inc=1, device_id={"cols": partner}, device_id_type=MESH)
    pl.semaphore_wait(barrier, 2 + chips)

    def to_peer(tick, j, i):
        return pltpu.make_async_remote_copy(
            src_ref=pack_ref.at[tick, i], dst_ref=gat.at[tick, col * per + i],
            send_sem=g_send.at[tick, j - 1, i], recv_sem=g_recv.at[tick, j - 1, i],
            device_id={"cols": peer_of(j)}, device_id_type=MESH)

    def to_partner(tick):
        return pltpu.make_async_remote_copy(
            src_ref=pack_ref.at[tick], dst_ref=share(tick, col),
            send_sem=p_send.at[tick], recv_sem=p_recv.at[tick],
            device_id={"cols": partner}, device_id_type=MESH)

    def forward(tick, j, i):
        owner = lax.rem(chip + chips - j, chips) * 2 + core
        return pltpu.make_async_remote_copy(
            src_ref=gat.at[tick, owner * per + i], dst_ref=gat.at[tick, owner * per + i],
            send_sem=f_send.at[tick, j - 1, i], recv_sem=f_recv.at[tick, j - 1, i],
            device_id={"cols": partner}, device_id_type=MESH)

    @pl.loop(0, ticks)
    def _(tick):
        @pl.loop(0, per)
        def _(m):
            for j in range(1, chips):
                to_peer(tick, j, per - 1 - m).start()
        to_partner(tick).start()
        own_copy(tick).start()

    ii = lax.broadcasted_iota(jnp.int32, (block, block), 0)
    jj = lax.broadcasted_iota(jnp.int32, (block, block), 1)
    unit = jnp.where(ii == jj, 1.0, 0.0).astype(f32)
    zero = jnp.zeros((block, block), f32)
    total_rows = work.shape[0]
    left, right = pl.ds(0, width), pl.ds(width, block)

    def reset():
        work[pl.ds(rows_here, total_rows - rows_here), :] = jnp.zeros(
            (total_rows - rows_here, width + block), f32)
        work[pl.ds(rows_here, block), right] = unit

    @pl.loop(0, rows_here // block)
    def _(i):
        work[pl.ds(pl.multiple_of(i * block, block), block), right] = zero

    reset()

    def in_block(tick, k):
        return start_ref[tick, k] - row * rows_here - k * block

    def prepare(tick, k):
        slot = tick * n_dia + k
        top = gat[tick, k, pl.ds(0, block), :]
        lower = jnp.where(ii < jj, 0.0, jnp.where(ii > jj, top, unit))
        fh, fl = split(jnp.where(ii <= jj, top, 0.0))
        house = jnp.concatenate(
            [lower, gat[tick, k, pl.ds(block, height - block), :],
             jnp.zeros((SHIFT, block), f32)], 0)
        house = pltpu.roll(house, in_block(tick, k), 0)
        high, low = split(house)
        wide = dot(jnp.concatenate([high, low], 1), jnp.concatenate([fh, fh], 0))
        wh, wl = split(wide + dot(high, fl))
        wcat[slot, :, pl.ds(0, block)] = wh
        wcat[slot, :, pl.ds(block, block)] = wl
        ah, al = split(house.T)
        vhi[slot] = ah
        vlo[slot] = al

    def prepare_share(tick, owner):
        @pl.loop(0, per, unroll=1)
        def _(i):
            prepare(tick, owner * per + i)

    def apply(tick, k):
        slot = tick * n_dia + k
        window = pl.ds(pl.multiple_of(k * block, block), reach)
        vh, vl, wc = vhi[slot], vlo[slot], wcat[slot]
        slab = work[window, :]
        sh, sl = split(slab)
        hb = block // 2
        proj = jnp.concatenate([
            dot(vh[p:p + hb], sh) + (dot(vl[p:p + hb], sh) + dot(vh[p:p + hb], sl))
            for p in (0, hb)], 0)
        ph, plow = split(proj)
        pp = jnp.concatenate([ph, ph], 0)
        hr = reach // 2
        for p in (0, hr):
            part = wc[p:p + hr]
            delta = dot(part, pp) + dot(part[:, :block], plow)
            work[pl.ds(pl.multiple_of(k * block, block) + p, hr), :] = slab[p:p + hr] - delta

    def send_up(tick, c):
        part = pl.ds(c * chunk, chunk)
        return pltpu.make_async_remote_copy(
            src_ref=outb.at[tick, part], dst_ref=inflow.at[tick, part],
            send_sem=i_send.at[tick, c], recv_sem=i_recv.at[tick, c],
            device_id={"rows": above}, device_id_type=MESH)

    def send_down(tick):
        return pltpu.make_async_remote_copy(
            src_ref=tailb.at[tick], dst_ref=head.at[tick],
            send_sem=h_send.at[tick], recv_sem=h_recv.at[tick],
            device_id={"rows": below}, device_id_type=MESH)

    def take_head(tick):
        send_down(tick).wait_recv()
        work[pl.ds(0, block), left] = head[tick]

    @pl.loop(0, 2 * ticks)
    def _(m):
        mine = m < ticks
        tick = jnp.where(mine, m, m - ticks)

        @pl.when(mine)
        def _():
            own_copy(tick).wait()

        @pl.when(jnp.logical_not(mine))
        def _():
            to_partner(tick).wait_recv()

        prepare_share(tick, jnp.where(mine, col, partner))

    vec_copy.wait()

    @pl.loop(0, ticks)
    def _(tick):
        @pl.loop(0, n_dia)
        def _(counter):
            k = n_dia - 1 - counter
            owner, i = lax.div(k, per), lax.rem(k, per)
            o_chip, o_core = lax.div(owner, 2), lax.rem(owner, 2)
            j = lax.rem(chip + chips - o_chip, chips)

            @pl.when(j > 0)
            def _():
                @pl.when(o_core == 1)
                def _():
                    to_peer(tick, j, i).wait_recv()
                    forward(tick, j, i).start()

                @pl.when(o_core != core)
                def _():
                    forward(tick, j, i).wait_recv()

                prepare(tick, k)

            @pl.when(jnp.logical_and(k == 0, jnp.logical_and(row > 0, tick > 0)))
            def _():
                take_head(jnp.maximum(tick - 1, 0))

            apply(tick, k)

        outb[tick] = work[pl.ds(0, block), left].T

        @pl.when(row == n_rows - 1)
        def _():
            for c in range(CHUNKS):
                send_up(tick, c).start()

        @pl.when(row < n_rows - 1)
        def _():
            mh, ml = split(work[pl.ds(0, block), right].T)
            for c in range(CHUNKS):
                send_up(tick, c).wait_recv()

                @pl.when(row > 0)
                def _():
                    part = pl.ds(c * chunk, chunk)
                    xh, xl = split(inflow[tick, part, :])
                    outb[tick, part, :] = outb[tick, part, :] + (
                        dot(xh, mh) + (dot(xl, mh) + dot(xh, ml)))
                    send_up(tick, c).start()

            flow = inflow[tick].T
            tail = pl.ds(rows_here, block)
            tailb[tick] = work[tail, left] + product(work[tail, right], flow)
            send_down(tick).start()
            fh, fl = split(flow)
            fcat = jnp.concatenate([fh, fh], 0)

            @pl.loop(0, rows_here // 256)
            def _(i):
                rows = pl.ds(pl.multiple_of(i * 256, 256), 256)
                rh, rl = split(work[rows, right])
                work[rows, left] = work[rows, left] + (
                    dot(jnp.concatenate([rh, rl], 1), fcat) + dot(rh, fl))

        @pl.when(tick < ticks - 1)
        def _():
            @pl.loop(0, rows_here // block)
            def _(i):
                work[pl.ds(pl.multiple_of(i * block, block), block), right] = zero
            reset()

    @pl.when(row > 0)
    def _():
        take_head(ticks - 1)

    out_copy = pltpu.make_async_copy(
        work.at[pl.ds(0, rows_here), pl.ds(0, width)], out_ref, vec_sem)
    out_copy.start()

    @pl.loop(0, ticks)
    def _(tick):
        @pl.loop(0, per)
        def _(i):
            for j in range(1, chips):
                to_peer(tick, j, i).wait_send()
                forward(tick, j, i).wait_send()
        to_partner(tick).wait_send()

        @pl.when(row > 0)
        def _():
            for c in range(CHUNKS):
                send_up(tick, c).wait_send()

        @pl.when(row < n_rows - 1)
        def _():
            send_down(tick).wait_send()

    out_copy.wait()


def solution(mesh):
    n_rows, n_cols = mesh.shape["rows"], mesh.shape["cols"]

    def on_device(vectors, reflectors, factors, starts):
        rows_here, width = vectors.shape
        ticks, per, height, block = reflectors.shape
        chips = n_cols // 2
        ii = lax.broadcasted_iota(jnp.int32, factors.shape, 2)
        jj = lax.broadcasted_iota(jnp.int32, factors.shape, 3)
        top = jnp.where(ii > jj, reflectors[:, :, :block], factors)
        packed = jnp.concatenate([top, reflectors[:, :, block:]], 2)
        dma = pltpu.SemaphoreType.DMA
        hops = max(chips - 1, 1)
        reach = height + SHIFT
        edge, flow = (ticks, block, width), (ticks, width, block)
        return pl.pallas_call(
            functools.partial(kernel, n_rows, n_cols),
            out_shape=jax.ShapeDtypeStruct(vectors.shape, f32),
            in_specs=[
                pl.BlockSpec(memory_space=pl.ANY),
                pl.BlockSpec(memory_space=pl.ANY),
                pl.BlockSpec(memory_space=pltpu.SMEM),
            ],
            out_specs=pl.BlockSpec(memory_space=pl.ANY),
            scratch_shapes=[
                pltpu.VMEM((ticks, per * n_cols, height, block), f32),
                pltpu.VMEM((rows_here + height - block + SHIFT, width + block), f32),
                pltpu.VMEM((ticks * per * n_cols, block, reach), bf16),
                pltpu.VMEM((ticks * per * n_cols, block, reach), bf16),
                pltpu.VMEM((ticks * per * n_cols, reach, 2 * block), bf16),
                pltpu.VMEM(flow, f32), pltpu.VMEM(edge, f32),
                pltpu.VMEM(flow, f32), pltpu.VMEM(edge, f32),
                dma, dma((ticks,)),
                dma((ticks, hops, per)), dma((ticks, hops, per)),
                dma((ticks,)), dma((ticks,)),
                dma((ticks, hops, per)), dma((ticks, hops, per)),
                dma((ticks, CHUNKS)), dma((ticks, CHUNKS)), dma((ticks,)), dma((ticks,)),
            ],
            compiler_params=pltpu.CompilerParams(
                collective_id=0, has_side_effects=True, vmem_limit_bytes=36 * 2**20),
        )(vectors, packed, starts)

    return jax.shard_map(
        on_device,
        mesh=mesh,
        in_specs=(
            P("rows", "cols"),
            P(None, ("rows", "cols"), None, None),
            P(None, ("rows", "cols"), None, None),
            P(None, "rows"),
        ),
        out_specs=P("rows", "cols"),
        check_vma=False,
    )
```

profile of v0, /device:TPU:0, one launch (start us, length us, event | category | flops | bytes accessed | tf_op | source)
XLA Modules:
  0.0 85.2 jit_solution(3559470932323433568)
XLA Ops:
  0.0 1.8 %slice_select_fusion = (f32[3,4,128,128]{3,2,1,0:T(8,128)S(1)}, f32[3,4,128,128]{3,2,1,0:T(8,128)S(1)}) fusion(f32[3,4,128,128]{3,2,1,0:T(8,128)} %param.6, f32[3,4,256,128]{3,2,1,0:T(8,128)} %param.5), kind=kLoop, calls=%fused_computation.1 | loop fusion | flops 393216 | bytes 3932160 | tf_op jit(solution)/shard_map/jit(_where)/select_n | solution.py:303
  1.8 0.0 copy-start
  1.8 0.0 copy-start.1
  1.8 0.1 pad_maximum_fusion.pack_ref
  1.9 1.1 %copy-done = f32[2048,128]{1,0:T(8,128)S(1)} copy-done((f32[2048,128]{1,0:T(8,128)S(1)}, f32[2048,128]{1,0:T(8,128)}, u32[]{:S(2)}) %copy-start) | copy-done | bytes 1048600
  3.0 0.0 copy-done.1
  3.0 81.2 %shard_map.46 = f32[2048,128]{1,0:T(8,128)S(1)} custom-call(f32[2048,128]{1,0:T(8,128)S(1)} %copy-done, f32[3,4,256,128]{3,2,1,0:T(8,128)S(1)} %pad_maximum_fusion.pack_ref, s32[3,16]{1,0:T(4,128)S(1)} %copy-done.1), custom_call_target="tpu_custom_call" | custom-call | tf_op jit(solution)/shard_map/pallas_call | solution.py:309
  84.2 1.0 %copy.6 = f32[2048,128]{1,0:T(8,128)} copy(f32[2048,128]{1,0:T(8,128)S(1)} %shard_map.46) | data formatting | bytes 2097152
Async XLA Ops:
  1.8 1.2 %copy-start = (f32[2048,128]{1,0:T(8,128)S(1)}, f32[2048,128]{1,0:T(8,128)}, u32[]{:S(2)}) copy-start(f32[2048,128]{1,0:T(8,128)} %vec_ref.1) | copy-start | bytes 3145732
  1.8 1.2 %copy-start.1 = (s32[3,16]{1,0:T(4,128)S(1)}, s32[3,16]{1,0:T(4,128)}, u32[]{:S(2)}) copy-start(s32[3,16]{1,0:T(4,128)} %start_ref.1) | copy-start | bytes 580
where the time goes:
time: 85.4 us; the launch traced here: 85.2 us
  Pallas kernels  81.2 us (95%)
  local copies, waits for them, and re-layouts  2.07 us (2%)
  other arithmetic  1.88 us (2%)
    pallas_call x1, Pallas kernels, on_device(): pl.pallas_call(functools.partial(kernel, n_rows, n_cols), out_shape=jax.S...  81.2 us
    unnamed x5, local copies, waits for them, and re-layouts  2.07 us
    select_n x1, other arithmetic, on_device(): top = jnp.where(ii > jj, reflectors[:, :, :block], factors)  1.76 us

commit v1 on v0

--- a/solution.py
+++ b/solution.py
@@ -22,18 +22,25 @@
     return jnp.dot(a, b, preferred_element_type=f32)
 
 
+def dot_nt(a, b):
+    return lax.dot_general(a, b, (((1,), (1,)), ((), ())), preferred_element_type=f32)
+
+
 def product(a, b):
+    return times(a, *split(b))
+
+
+def times(a, bh, bl):
     ah, al = split(a)
-    bh, bl = split(b)
     return dot(ah, bh) + (dot(al, bh) + dot(ah, bl))
 
 
 def kernel(
     n_rows, n_cols,
     vec_ref, pack_ref, start_ref, out_ref,
-    gat, work, vhi, vlo, wcat, inflow, head, outb, tailb,
+    gat, work, dense, shifted, inflow, head, outb, tailb, topb, lowb,
     vec_sem, own_sem, g_send, g_recv, p_send, p_recv, f_send, f_recv,
-    i_send, i_recv, h_send, h_recv,
+    i_send, j_send, i_recv, h_send, h_recv, t_send, t_recv,
 ):
     row = lax.axis_index("rows")
     col = lax.axis_index("cols")
@@ -46,6 +53,9 @@
     chip, core = lax.div(col, 2), lax.rem(col, 2)
     partner = chip * 2 + 1 - core
     above, below = lax.rem(row + n_rows - 1, n_rows), lax.rem(row + 1, n_rows)
+    above2, below2 = lax.rem(row + n_rows - 2, n_rows), lax.rem(row + 2, n_rows)
+    upper = lax.rem(row, 2) == 0
+    last_pair = row >= n_rows - 2
 
     def peer_of(j):
         return lax.rem(chip + j, chips) * 2 + core
@@ -54,19 +64,19 @@
         return gat.at[tick, pl.ds(owner * per, per)]
 
     vec_copy = pltpu.make_async_copy(
-        vec_ref, work.at[pl.ds(0, rows_here), pl.ds(0, width)], vec_sem)
+        vec_ref, work.at[0, pl.ds(0, rows_here)], vec_sem)
     vec_copy.start()
 
     def own_copy(tick):
         return pltpu.make_async_copy(pack_ref.at[tick], share(tick, col), own_sem.at[tick])
 
     barrier = pltpu.get_barrier_semaphore()
-    for there in (above, below):
+    for there in (above, below, above2, below2):
         pl.semaphore_signal(barrier, inc=1, device_id={"rows": there}, device_id_type=MESH)
     for j in range(1, chips):
         pl.semaphore_signal(barrier, inc=1, device_id={"cols": peer_of(j)}, device_id_type=MESH)
     pl.semaphore_signal(barrier, inc=1, device_id={"cols": partner}, device_id_type=MESH)
-    pl.semaphore_wait(barrier, 2 + chips)
+    pl.semaphore_wait(barrier, 4 + chips)
 
     def to_peer(tick, j, i):
         return pltpu.make_async_remote_copy(
@@ -100,40 +110,38 @@
     jj = lax.broadcasted_iota(jnp.int32, (block, block), 1)
     unit = jnp.where(ii == jj, 1.0, 0.0).astype(f32)
     zero = jnp.zeros((block, block), f32)
-    total_rows = work.shape[0]
-    left, right = pl.ds(0, width), pl.ds(width, block)
+    total_rows = work.shape[1]
 
     def reset():
-        work[pl.ds(rows_here, total_rows - rows_here), :] = jnp.zeros(
-            (total_rows - rows_here, width + block), f32)
-        work[pl.ds(rows_here, block), right] = unit
-
-    @pl.loop(0, rows_here // block)
-    def _(i):
-        work[pl.ds(pl.multiple_of(i * block, block), block), right] = zero
-
+        spare = total_rows - rows_here
+        work[:, pl.ds(rows_here, spare), :] = jnp.zeros((2, spare, block), f32)
+        work[1, pl.ds(rows_here, block), :] = unit
+
+    def clear_right():
+        @pl.loop(0, rows_here // block)
+        def _(i):
+            work[1, pl.ds(pl.multiple_of(i * block, block), block), :] = zero
+
+    clear_right()
     reset()
+    shifted[...] = jnp.zeros_like(shifted)
 
     def in_block(tick, k):
-        return start_ref[tick, k] - row * rows_here - k * block
+        return jnp.clip(start_ref[tick, k] - row * rows_here - k * block, 0, SHIFT)
 
     def prepare(tick, k):
         slot = tick * n_dia + k
         top = gat[tick, k, pl.ds(0, block), :]
         lower = jnp.where(ii < jj, 0.0, jnp.where(ii > jj, top, unit))
         fh, fl = split(jnp.where(ii <= jj, top, 0.0))
-        house = jnp.concatenate(
-            [lower, gat[tick, k, pl.ds(block, height - block), :],
-             jnp.zeros((SHIFT, block), f32)], 0)
-        house = pltpu.roll(house, in_block(tick, k), 0)
+        house = jnp.concatenate([lower, gat[tick, k, pl.ds(block, height - block), :]], 0)
         high, low = split(house)
         wide = dot(jnp.concatenate([high, low], 1), jnp.concatenate([fh, fh], 0))
         wh, wl = split(wide + dot(high, fl))
-        wcat[slot, :, pl.ds(0, block)] = wh
-        wcat[slot, :, pl.ds(block, block)] = wl
-        ah, al = split(house.T)
-        vhi[slot] = ah
-        vlo[slot] = al
+        full = dot_nt(jnp.concatenate([wh, wl], 1), jnp.concatenate([high, high], 1))
+        dh, dl = split(full + dot_nt(wh, low))
+        dense[slot, pl.ds(0, height)] = dh
+        dense[slot, pl.ds(height, height)] = dl
 
     def prepare_share(tick, owner):
         @pl.loop(0, per, unroll=1)
@@ -142,27 +150,36 @@
 
     def apply(tick, k):
         slot = tick * n_dia + k
-        window = pl.ds(pl.multiple_of(k * block, block), reach)
-        vh, vl, wc = vhi[slot], vlo[slot], wcat[slot]
-        slab = work[window, :]
+        shift = in_block(tick, k)
+        base = pl.multiple_of(k * block, block)
+        slab = jnp.concatenate([work[h, pl.ds(base + shift, height), :] for h in (0, 1)], 1)
         sh, sl = split(slab)
-        hb = block // 2
-        proj = jnp.concatenate([
-            dot(vh[p:p + hb], sh) + (dot(vl[p:p + hb], sh) + dot(vh[p:p + hb], sl))
-            for p in (0, hb)], 0)
-        ph, plow = split(proj)
-        pp = jnp.concatenate([ph, ph], 0)
-        hr = reach // 2
-        for p in (0, hr):
-            part = wc[p:p + hr]
-            delta = dot(part, pp) + dot(part[:, :block], plow)
-            work[pl.ds(pl.multiple_of(k * block, block) + p, hr), :] = slab[p:p + hr] - delta
-
-    def send_up(tick, c):
+        half = height // 2
+        delta = jnp.concatenate([
+            dot(dense[slot, pl.ds(p, half)], sh)
+            + (dot(dense[slot, pl.ds(height + p, half)], sh) + dot(dense[slot, pl.ds(p, half)], sl))
+            for p in (0, half)], 0)
+        for h in (0, 1):
+            shifted[h, pl.ds(SHIFT, height), :] = delta[:, h * block:(h + 1) * block]
+        for h in (0, 1):
+            work[h, pl.ds(base, reach), :] = (
+                work[h, pl.ds(base, reach), :] - shifted[h, pl.ds(SHIFT - shift, reach), :])
+
+    def send_up(tick, c, there, sems):
         part = pl.ds(c * chunk, chunk)
         return pltpu.make_async_remote_copy(
             src_ref=outb.at[tick, part], dst_ref=inflow.at[tick, part],
-            send_sem=i_send.at[tick, c], recv_sem=i_recv.at[tick, c],
+            send_sem=sems.at[tick, c], recv_sem=i_recv.at[tick, c],
+            device_id={"rows": there}, device_id_type=MESH)
+
+    def start_up(tick, c):
+        send_up(tick, c, above2, i_send).start()
+        send_up(tick, c, above, j_send).start()
+
+    def pair_up(tick, m):
+        return pltpu.make_async_remote_copy(
+            src_ref=topb.at[tick, m], dst_ref=lowb.at[tick, m],
+            send_sem=t_send.at[tick, m], recv_sem=t_recv.at[tick, m],
             device_id={"rows": above}, device_id_type=MESH)
 
     def send_down(tick):
@@ -173,7 +190,7 @@
 
     def take_head(tick):
         send_down(tick).wait_recv()
-        work[pl.ds(0, block), left] = head[tick]
+        work[0, pl.ds(0, block), :] = head[tick]
 
     @pl.loop(0, 2 * ticks)
     def _(m):
@@ -220,46 +237,71 @@
 
             apply(tick, k)
 
-        outb[tick] = work[pl.ds(0, block), left].T
-
-        @pl.when(row == n_rows - 1)
-        def _():
-            for c in range(CHUNKS):
-                send_up(tick, c).start()
-
-        @pl.when(row < n_rows - 1)
-        def _():
-            mh, ml = split(work[pl.ds(0, block), right].T)
-            for c in range(CHUNKS):
-                send_up(tick, c).wait_recv()
-
-                @pl.when(row > 0)
-                def _():
-                    part = pl.ds(c * chunk, chunk)
-                    xh, xl = split(inflow[tick, part, :])
-                    outb[tick, part, :] = outb[tick, part, :] + (
-                        dot(xh, mh) + (dot(xl, mh) + dot(xh, ml)))
-                    send_up(tick, c).start()
-
-            flow = inflow[tick].T
+        edge = pl.ds(0, block)
+
+        def correct(flow):
             tail = pl.ds(rows_here, block)
-            tailb[tick] = work[tail, left] + product(work[tail, right], flow)
+            fh, fl = split(flow)
+            tailb[tick] = work[0, tail, :] + times(work[1, tail, :], fh, fl)
             send_down(tick).start()
-            fh, fl = split(flow)
             fcat = jnp.concatenate([fh, fh], 0)
 
             @pl.loop(0, rows_here // 256)
             def _(i):
                 rows = pl.ds(pl.multiple_of(i * 256, 256), 256)
-                rh, rl = split(work[rows, right])
-                work[rows, left] = work[rows, left] + (
+                rh, rl = split(work[1, rows, :])
+                work[0, rows, :] = work[0, rows, :] + (
                     dot(jnp.concatenate([rh, rl], 1), fcat) + dot(rh, fl))
 
+        @pl.when(jnp.logical_not(upper))
+        def _():
+            for m in (0, 1):
+                topb[tick, m] = work[m, edge, :].T
+            for m in (0, 1):
+                pair_up(tick, m).start()
+
+            @pl.when(jnp.logical_not(last_pair))
+            def _():
+                for c in range(CHUNKS):
+                    send_up(tick, c, above, j_send).wait_recv()
+                correct(inflow[tick].T)
+
+        @pl.when(upper)
+        def _():
+            mh, ml = split(work[1, edge, :].T)
+            outb[tick] = work[0, edge, :].T
+            pair_up(tick, 0).wait_recv()
+            outb[tick] = outb[tick] + times(lowb[tick, 0], mh, ml)
+
+            @pl.when(last_pair)
+            def _():
+                @pl.when(row > 0)
+                def _():
+                    for c in range(CHUNKS):
+                        start_up(tick, c)
+                pair_up(tick, 1).wait_recv()
+                correct(lowb[tick, 0].T)
+
+            @pl.when(jnp.logical_not(last_pair))
+            def _():
+                pair_up(tick, 1).wait_recv()
+                nh, nl = split(times(lowb[tick, 1], mh, ml))
+                for c in range(CHUNKS):
+                    send_up(tick, c, above2, i_send).wait_recv()
+
+                    @pl.when(row > 0)
+                    def _():
+                        part = pl.ds(c * chunk, chunk)
+                        outb[tick, part, :] = outb[tick, part, :] + times(
+                            inflow[tick, part, :], nh, nl)
+                        start_up(tick, c)
+
+                lh, ll = split(lowb[tick, 1])
+                correct((lowb[tick, 0] + times(inflow[tick], lh, ll)).T)
+
         @pl.when(tick < ticks - 1)
         def _():
-            @pl.loop(0, rows_here // block)
-            def _(i):
-                work[pl.ds(pl.multiple_of(i * block, block), block), right] = zero
+            clear_right()
             reset()
 
     @pl.when(row > 0)
@@ -267,7 +309,7 @@
         take_head(ticks - 1)
 
     out_copy = pltpu.make_async_copy(
-        work.at[pl.ds(0, rows_here), pl.ds(0, width)], out_ref, vec_sem)
+        work.at[0, pl.ds(0, rows_here)], out_ref, vec_sem)
     out_copy.start()
 
     @pl.loop(0, ticks)
@@ -279,10 +321,16 @@
                 forward(tick, j, i).wait_send()
         to_partner(tick).wait_send()
 
-        @pl.when(row > 0)
+        @pl.when(jnp.logical_and(upper, row > 0))
         def _():
             for c in range(CHUNKS):
-                send_up(tick, c).wait_send()
+                send_up(tick, c, above2, i_send).wait_send()
+                send_up(tick, c, above, j_send).wait_send()
+
+        @pl.when(jnp.logical_not(upper))
+        def _():
+            for m in (0, 1):
+                pair_up(tick, m).wait_send()
 
         @pl.when(row < n_rows - 1)
         def _():
@@ -304,7 +352,6 @@
         packed = jnp.concatenate([top, reflectors[:, :, block:]], 2)
         dma = pltpu.SemaphoreType.DMA
         hops = max(chips - 1, 1)
-        reach = height + SHIFT
         edge, flow = (ticks, block, width), (ticks, width, block)
         return pl.pallas_call(
             functools.partial(kernel, n_rows, n_cols),
@@ -317,17 +364,19 @@
             out_specs=pl.BlockSpec(memory_space=pl.ANY),
             scratch_shapes=[
                 pltpu.VMEM((ticks, per * n_cols, height, block), f32),
-                pltpu.VMEM((rows_here + height - block + SHIFT, width + block), f32),
-                pltpu.VMEM((ticks * per * n_cols, block, reach), bf16),
-                pltpu.VMEM((ticks * per * n_cols, block, reach), bf16),
-                pltpu.VMEM((ticks * per * n_cols, reach, 2 * block), bf16),
+                pltpu.VMEM((2, rows_here + height - block + SHIFT, block), f32),
+                pltpu.VMEM((ticks * per * n_cols, 2 * height, height), bf16),
+                pltpu.VMEM((2, height + 2 * SHIFT, block), f32),
                 pltpu.VMEM(flow, f32), pltpu.VMEM(edge, f32),
                 pltpu.VMEM(flow, f32), pltpu.VMEM(edge, f32),
+                pltpu.VMEM((ticks, 2, block, block), f32),
+                pltpu.VMEM((ticks, 2, block, block), f32),
                 dma, dma((ticks,)),
                 dma((ticks, hops, per)), dma((ticks, hops, per)),
                 dma((ticks,)), dma((ticks,)),
                 dma((ticks, hops, per)), dma((ticks, hops, per)),
-                dma((ticks, CHUNKS)), dma((ticks, CHUNKS)), dma((ticks,)), dma((ticks,)),
+                dma((ticks, CHUNKS)), dma((ticks, CHUNKS)), dma((ticks, CHUNKS)),
+                dma((ticks,)), dma((ticks,)), dma((ticks, 2)), dma((ticks, 2)),
             ],
             compiler_params=pltpu.CompilerParams(
                 collective_id=0, has_side_effects=True, vmem_limit_bytes=36 * 2**20),

time: 85.4 us -> 79.1 us (0.926)
  Pallas kernels: 81.2 us -> 74.5 us
    pallas_call x1, Pallas kernels: 81.2 us -> 74.5 us  [on_device(): pl.pallas_call(functools.partial(kernel, n_rows, n_cols), out_shape=jax.S...]
where the time goes in v1:
time: 79.1 us; the launch traced here: 78.5 us
  Pallas kernels  74.5 us (94%)
  local copies, waits for them, and re-layouts  2.07 us (3%)
  other arithmetic  1.88 us (2%)
    pallas_call x1, Pallas kernels, on_device(): pl.pallas_call(functools.partial(kernel, n_rows, n_cols), out_shape=jax.S...  74.5 us
    unnamed x5, local copies, waits for them, and re-layouts  2.07 us
    select_n x1, other arithmetic, on_device(): top = jnp.where(ii > jj, reflectors[:, :, :block], factors)  1.76 us

profile of v1, /device:TPU:0, one launch (start us, length us, event | category | flops | bytes accessed | tf_op | source)
XLA Modules:
  0.0 78.5 jit_solution(18087498939787910122)
XLA Ops:
  0.0 1.8 %slice_select_fusion = (f32[3,4,128,128]{3,2,1,0:T(8,128)S(1)}, f32[3,4,128,128]{3,2,1,0:T(8,128)S(1)}) fusion(f32[3,4,128,128]{3,2,1,0:T(8,128)} %param.6, f32[3,4,256,128]{3,2,1,0:T(8,128)} %param.5), kind=kLoop, calls=%fused_computation.1 | loop fusion | flops 393216 | bytes 3932160 | tf_op jit(solution)/shard_map/jit(_where)/select_n | solution.py:351
  1.8 0.0 copy-start
  1.8 0.0 copy-start.1
  1.8 0.1 pad_maximum_fusion.pack_ref
  1.9 1.1 %copy-done = f32[2048,128]{1,0:T(8,128)S(1)} copy-done((f32[2048,128]{1,0:T(8,128)S(1)}, f32[2048,128]{1,0:T(8,128)}, u32[]{:S(2)}) %copy-start) | copy-done | bytes 1048600
  3.0 0.0 copy-done.1
  3.0 74.5 %shard_map.46 = f32[2048,128]{1,0:T(8,128)S(1)} custom-call(f32[2048,128]{1,0:T(8,128)S(1)} %copy-done, f32[3,4,256,128]{3,2,1,0:T(8,128)S(1)} %pad_maximum_fusion.pack_ref, s32[3,16]{1,0:T(4,128)S(1)} %copy-done.1), custom_call_target="tpu_custom_call" | custom-call | tf_op jit(solution)/shard_map/pallas_call | solution.py:356
  77.5 1.0 %copy.6 = f32[2048,128]{1,0:T(8,128)} copy(f32[2048,128]{1,0:T(8,128)S(1)} %shard_map.46) | data formatting | bytes 2097152
Async XLA Ops:
  1.8 1.2 %copy-start = (f32[2048,128]{1,0:T(8,128)S(1)}, f32[2048,128]{1,0:T(8,128)}, u32[]{:S(2)}) copy-start(f32[2048,128]{1,0:T(8,128)} %vec_ref.1) | copy-start | bytes 3145732
  1.8 1.2 %copy-start.1 = (s32[3,16]{1,0:T(4,128)S(1)}, s32[3,16]{1,0:T(4,128)}, u32[]{:S(2)}) copy-start(s32[3,16]{1,0:T(4,128)} %start_ref.1) | copy-start | bytes 580

commit v2 on v1

--- a/solution.py
+++ b/solution.py
@@ -9,7 +9,7 @@
 
 MESH = pl.DeviceIdType.MESH
 SHIFT = 64
-CHUNKS = 4
+CHUNKS = 2
 f32, bf16 = jnp.float32, jnp.bfloat16
 
 
@@ -37,14 +37,14 @@
 
 def kernel(
     n_rows, n_cols,
-    vec_ref, pack_ref, start_ref, out_ref,
-    gat, work, dense, shifted, inflow, head, outb, tailb, topb, lowb,
-    vec_sem, own_sem, g_send, g_recv, p_send, p_recv, f_send, f_recv,
+    vec_ref, refl_ref, fact_ref, start_ref, out_ref,
+    gat, fact, work, dense, shifted, inflow, head, outb, tailb, topb, lowb, both,
+    vec_sem, own_sem, fact_sem, g_send, g_recv, p_send, p_recv, f_send, f_recv,
     i_send, j_send, i_recv, h_send, h_recv, t_send, t_recv,
 ):
     row = lax.axis_index("rows")
     col = lax.axis_index("cols")
-    ticks, per, height, block = pack_ref.shape
+    ticks, per, height, block = refl_ref.shape
     rows_here, width = vec_ref.shape
     n_dia = per * n_cols
     reach = height + SHIFT
@@ -65,10 +65,19 @@
 
     vec_copy = pltpu.make_async_copy(
         vec_ref, work.at[0, pl.ds(0, rows_here)], vec_sem)
+
+    def own_copy(tick):
+        return pltpu.make_async_copy(refl_ref.at[tick], share(tick, col), own_sem.at[tick])
+
+    def fact_copy(tick):
+        return pltpu.make_async_copy(fact_ref.at[tick], fact.at[tick], fact_sem.at[tick])
+
+    @pl.loop(0, ticks)
+    def _(tick):
+        own_copy(tick).start()
+        fact_copy(tick).start()
+
     vec_copy.start()
-
-    def own_copy(tick):
-        return pltpu.make_async_copy(pack_ref.at[tick], share(tick, col), own_sem.at[tick])
 
     barrier = pltpu.get_barrier_semaphore()
     for there in (above, below, above2, below2):
@@ -80,13 +89,13 @@
 
     def to_peer(tick, j, i):
         return pltpu.make_async_remote_copy(
-            src_ref=pack_ref.at[tick, i], dst_ref=gat.at[tick, col * per + i],
+            src_ref=gat.at[tick, col * per + i], dst_ref=gat.at[tick, col * per + i],
             send_sem=g_send.at[tick, j - 1, i], recv_sem=g_recv.at[tick, j - 1, i],
             device_id={"cols": peer_of(j)}, device_id_type=MESH)
 
     def to_partner(tick):
         return pltpu.make_async_remote_copy(
-            src_ref=pack_ref.at[tick], dst_ref=share(tick, col),
+            src_ref=share(tick, col), dst_ref=share(tick, col),
             send_sem=p_send.at[tick], recv_sem=p_recv.at[tick],
             device_id={"cols": partner}, device_id_type=MESH)
 
@@ -97,19 +106,28 @@
             send_sem=f_send.at[tick, j - 1, i], recv_sem=f_recv.at[tick, j - 1, i],
             device_id={"cols": partner}, device_id_type=MESH)
 
+    ii = lax.broadcasted_iota(jnp.int32, (block, block), 0)
+    jj = lax.broadcasted_iota(jnp.int32, (block, block), 1)
+    unit = jnp.where(ii == jj, 1.0, 0.0).astype(f32)
+    zero = jnp.zeros((block, block), f32)
+
     @pl.loop(0, ticks)
     def _(tick):
+        own_copy(tick).wait()
+        fact_copy(tick).wait()
+
+        @pl.loop(0, per)
+        def _(m):
+            k = col * per + per - 1 - m
+            gat[tick, k, pl.ds(0, block), :] = jnp.where(
+                ii > jj, gat[tick, k, pl.ds(0, block), :], fact[tick, per - 1 - m])
+
         @pl.loop(0, per)
         def _(m):
             for j in range(1, chips):
                 to_peer(tick, j, per - 1 - m).start()
         to_partner(tick).start()
-        own_copy(tick).start()
-
-    ii = lax.broadcasted_iota(jnp.int32, (block, block), 0)
-    jj = lax.broadcasted_iota(jnp.int32, (block, block), 1)
-    unit = jnp.where(ii == jj, 1.0, 0.0).astype(f32)
-    zero = jnp.zeros((block, block), f32)
+
     total_rows = work.shape[1]
 
     def reset():
@@ -192,21 +210,16 @@
         send_down(tick).wait_recv()
         work[0, pl.ds(0, block), :] = head[tick]
 
-    @pl.loop(0, 2 * ticks)
-    def _(m):
-        mine = m < ticks
-        tick = jnp.where(mine, m, m - ticks)
-
-        @pl.when(mine)
-        def _():
-            own_copy(tick).wait()
-
-        @pl.when(jnp.logical_not(mine))
-        def _():
-            to_partner(tick).wait_recv()
-
-        prepare_share(tick, jnp.where(mine, col, partner))
-
+    def prepare_own(tick):
+        @pl.loop(0, 2)
+        def _(m):
+            @pl.when(m == 1)
+            def _():
+                to_partner(tick).wait_recv()
+
+            prepare_share(tick, jnp.where(m == 0, col, partner))
+
+    prepare_own(0)
     vec_copy.wait()
 
     @pl.loop(0, ticks)
@@ -246,12 +259,15 @@
             send_down(tick).start()
             fcat = jnp.concatenate([fh, fh], 0)
 
-            @pl.loop(0, rows_here // 256)
+            span = 4 * block
+
+            @pl.loop(0, rows_here // span)
             def _(i):
-                rows = pl.ds(pl.multiple_of(i * 256, 256), 256)
+                rows = pl.ds(pl.multiple_of(i * span, span), span)
                 rh, rl = split(work[1, rows, :])
                 work[0, rows, :] = work[0, rows, :] + (
                     dot(jnp.concatenate([rh, rl], 1), fcat) + dot(rh, fl))
+                work[1, rows, :] = jnp.zeros((span, block), f32)
 
         @pl.when(jnp.logical_not(upper))
         def _():
@@ -260,12 +276,6 @@
             for m in (0, 1):
                 pair_up(tick, m).start()
 
-            @pl.when(jnp.logical_not(last_pair))
-            def _():
-                for c in range(CHUNKS):
-                    send_up(tick, c, above, j_send).wait_recv()
-                correct(inflow[tick].T)
-
         @pl.when(upper)
         def _():
             mh, ml = split(work[1, edge, :].T)
@@ -273,19 +283,39 @@
             pair_up(tick, 0).wait_recv()
             outb[tick] = outb[tick] + times(lowb[tick, 0], mh, ml)
 
+            @pl.when(jnp.logical_and(last_pair, row > 0))
+            def _():
+                for c in range(CHUNKS):
+                    start_up(tick, c)
+
+            pair_up(tick, 1).wait_recv()
+            both[...] = times(lowb[tick, 1], mh, ml)
+
+        @pl.when(tick < ticks - 1)
+        def _():
+            prepare_own(jnp.minimum(tick + 1, ticks - 1))
+
+        @pl.when(jnp.logical_not(upper))
+        def _():
             @pl.when(last_pair)
             def _():
-                @pl.when(row > 0)
-                def _():
-                    for c in range(CHUNKS):
-                        start_up(tick, c)
-                pair_up(tick, 1).wait_recv()
+                clear_right()
+
+            @pl.when(jnp.logical_not(last_pair))
+            def _():
+                for c in range(CHUNKS):
+                    send_up(tick, c, above, j_send).wait_recv()
+                correct(inflow[tick].T)
+
+        @pl.when(upper)
+        def _():
+            @pl.when(last_pair)
+            def _():
                 correct(lowb[tick, 0].T)
 
             @pl.when(jnp.logical_not(last_pair))
             def _():
-                pair_up(tick, 1).wait_recv()
-                nh, nl = split(times(lowb[tick, 1], mh, ml))
+                nh, nl = split(both[...])
                 for c in range(CHUNKS):
                     send_up(tick, c, above2, i_send).wait_recv()
 
@@ -301,7 +331,6 @@
 
         @pl.when(tick < ticks - 1)
         def _():
-            clear_right()
             reset()
 
     @pl.when(row > 0)
@@ -346,10 +375,6 @@
         rows_here, width = vectors.shape
         ticks, per, height, block = reflectors.shape
         chips = n_cols // 2
-        ii = lax.broadcasted_iota(jnp.int32, factors.shape, 2)
-        jj = lax.broadcasted_iota(jnp.int32, factors.shape, 3)
-        top = jnp.where(ii > jj, reflectors[:, :, :block], factors)
-        packed = jnp.concatenate([top, reflectors[:, :, block:]], 2)
         dma = pltpu.SemaphoreType.DMA
         hops = max(chips - 1, 1)
         edge, flow = (ticks, block, width), (ticks, width, block)
@@ -359,11 +384,13 @@
             in_specs=[
                 pl.BlockSpec(memory_space=pl.ANY),
                 pl.BlockSpec(memory_space=pl.ANY),
+                pl.BlockSpec(memory_space=pl.ANY),
                 pl.BlockSpec(memory_space=pltpu.SMEM),
             ],
             out_specs=pl.BlockSpec(memory_space=pl.ANY),
             scratch_shapes=[
                 pltpu.VMEM((ticks, per * n_cols, height, block), f32),
+                pltpu.VMEM((ticks, per, block, block), f32),
                 pltpu.VMEM((2, rows_here + height - block + SHIFT, block), f32),
                 pltpu.VMEM((ticks * per * n_cols, 2 * height, height), bf16),
                 pltpu.VMEM((2, height + 2 * SHIFT, block), f32),
@@ -371,7 +398,8 @@
                 pltpu.VMEM(flow, f32), pltpu.VMEM(edge, f32),
                 pltpu.VMEM((ticks, 2, block, block), f32),
                 pltpu.VMEM((ticks, 2, block, block), f32),
-                dma, dma((ticks,)),
+                pltpu.VMEM((block, block), f32),
+                dma, dma((ticks,)), dma((ticks,)),
                 dma((ticks, hops, per)), dma((ticks, hops, per)),
                 dma((ticks,)), dma((ticks,)),
                 dma((ticks, hops, per)), dma((ticks, hops, per)),
@@ -379,8 +407,8 @@
                 dma((ticks,)), dma((ticks,)), dma((ticks, 2)), dma((ticks, 2)),
             ],
             compiler_params=pltpu.CompilerParams(
-                collective_id=0, has_side_effects=True, vmem_limit_bytes=36 * 2**20),
-        )(vectors, packed, starts)
+                collective_id=0, has_side_effects=True, vmem_limit_bytes=63 * 2**20),
+        )(vectors, reflectors, factors, starts)
 
     return jax.shard_map(
         on_device,

time: 79.1 us -> 80.4 us (1.016)
  Pallas kernels: 74.5 us -> 76.8 us
  other arithmetic: 1.88 us -> 0 us
    pallas_call x1, Pallas kernels: 74.5 us -> 76.8 us  [on_device(): pl.pallas_call(functools.partial(kernel, n_rows, n_cols), out_shape=jax.S...]
    select_n x1 -> x0, other arithmetic: 1.76 us -> none  [on_device(): top = jnp.where(ii > jj, reflectors[:, :, :block], factors)]
    unnamed x5 -> x1, local copies, waits for them, and re-layouts: 2.07 us -> 2.26 us
where the time goes in v2:
time: 80.4 us; the launch traced here: 79 us
  Pallas kernels  76.8 us (96%)
  local copies, waits for them, and re-layouts  2.26 us (3%)
    pallas_call x1, Pallas kernels, on_device(): pl.pallas_call(functools.partial(kernel, n_rows, n_cols), out_shape=jax.S...  76.8 us
    unnamed x1, local copies, waits for them, and re-layouts  2.26 us

profile of v2, /device:TPU:0, one launch (start us, length us, event | category | flops | bytes accessed | tf_op | source)
XLA Modules:
  0.0 79.0 jit_solution(13828085753316891068)
XLA Ops:
  0.0 76.8 %shard_map.46 = f32[2048,128]{1,0:T(8,128)} custom-call(f32[2048,128]{1,0:T(8,128)} %vec_ref.1, f32[3,4,256,128]{3,2,1,0:T(8,128)} %refl_ref.1, f32[3,4,128,128]{3,2,1,0:T(8,128)} %fact_ref.1, s32[3,16]{1,0:T(4,128)} %start_ref.1), custom_call_target="tpu_custom_call" | custom-call | tf_op jit(solution)/shard_map/pallas_call | solution.py:381
  76.8 2.3 %copy.6 = f32[2048,128]{1,0:T(8,128)} copy(f32[2048,128]{1,0:T(8,128)} %shard_map.46) | data formatting | bytes 2097152

commit v3 on v2

--- a/solution.py
+++ b/solution.py
@@ -162,7 +162,7 @@
         dense[slot, pl.ds(height, height)] = dl
 
     def prepare_share(tick, owner):
-        @pl.loop(0, per, unroll=1)
+        @pl.loop(0, per, unroll=2 if per % 2 == 0 else 1)
         def _(i):
             prepare(tick, owner * per + i)
 
@@ -190,25 +190,23 @@
             send_sem=sems.at[tick, c], recv_sem=i_recv.at[tick, c],
             device_id={"rows": there}, device_id_type=MESH)
 
-    def start_up(tick, c):
-        send_up(tick, c, above2, i_send).start()
-        send_up(tick, c, above, j_send).start()
-
     def pair_up(tick, m):
         return pltpu.make_async_remote_copy(
             src_ref=topb.at[tick, m], dst_ref=lowb.at[tick, m],
             send_sem=t_send.at[tick, m], recv_sem=t_recv.at[tick, m],
             device_id={"rows": above}, device_id_type=MESH)
 
-    def send_down(tick):
-        return pltpu.make_async_remote_copy(
-            src_ref=tailb.at[tick], dst_ref=head.at[tick],
-            send_sem=h_send.at[tick], recv_sem=h_recv.at[tick],
+    def send_down(tick, m):
+        return pltpu.make_async_remote_copy(
+            src_ref=tailb.at[tick, m], dst_ref=head.at[tick, m],
+            send_sem=h_send.at[tick, m], recv_sem=h_recv.at[tick, m],
             device_id={"rows": below}, device_id_type=MESH)
 
     def take_head(tick):
-        send_down(tick).wait_recv()
-        work[0, pl.ds(0, block), :] = head[tick]
+        for m in (0, 1):
+            send_down(tick, m).wait_recv()
+        edge = pl.ds(0, block)
+        work[0, edge, :] = head[tick, 0] + product(head[tick, 1], work[0, edge, :])
 
     def prepare_own(tick):
         @pl.loop(0, 2)
@@ -224,39 +222,57 @@
 
     @pl.loop(0, ticks)
     def _(tick):
+        def turns(k):
+            return lax.rem(chip + chips - lax.div(lax.div(k, per), 2), chips)
+
+        def fetch(k):
+            owner, i = lax.div(k, per), lax.rem(k, per)
+            o_core = lax.rem(owner, 2)
+            j = turns(k)
+
+            @pl.when(o_core == 1)
+            def _():
+                to_peer(tick, j, i).wait_recv()
+                forward(tick, j, i).start()
+
+            @pl.when(o_core != core)
+            def _():
+                forward(tick, j, i).wait_recv()
+
+        @pl.when(turns(n_dia - 1) > 0)
+        def _():
+            fetch(n_dia - 1)
+            prepare(tick, n_dia - 1)
+
         @pl.loop(0, n_dia)
         def _(counter):
             k = n_dia - 1 - counter
-            owner, i = lax.div(k, per), lax.rem(k, per)
-            o_chip, o_core = lax.div(owner, 2), lax.rem(owner, 2)
-            j = lax.rem(chip + chips - o_chip, chips)
-
-            @pl.when(j > 0)
-            def _():
-                @pl.when(o_core == 1)
-                def _():
-                    to_peer(tick, j, i).wait_recv()
-                    forward(tick, j, i).start()
-
-                @pl.when(o_core != core)
-                def _():
-                    forward(tick, j, i).wait_recv()
-
-                prepare(tick, k)
+            later = jnp.maximum(k - 1, 0)
+            ahead = jnp.logical_and(k > 0, turns(later) > 0)
+
+            @pl.when(ahead)
+            def _():
+                fetch(later)
 
             @pl.when(jnp.logical_and(k == 0, jnp.logical_and(row > 0, tick > 0)))
             def _():
                 take_head(jnp.maximum(tick - 1, 0))
 
-            apply(tick, k)
+            @pl.when(ahead)
+            def _():
+                apply(tick, k)
+                prepare(tick, later)
+
+            @pl.when(jnp.logical_not(ahead))
+            def _():
+                apply(tick, k)
 
         edge = pl.ds(0, block)
+        for m in (0, 1):
+            tailb[tick, m] = work[m, pl.ds(rows_here, block), :]
 
         def correct(flow):
-            tail = pl.ds(rows_here, block)
             fh, fl = split(flow)
-            tailb[tick] = work[0, tail, :] + times(work[1, tail, :], fh, fl)
-            send_down(tick).start()
             fcat = jnp.concatenate([fh, fh], 0)
 
             span = 4 * block
@@ -286,10 +302,17 @@
             @pl.when(jnp.logical_and(last_pair, row > 0))
             def _():
                 for c in range(CHUNKS):
-                    start_up(tick, c)
+                    send_up(tick, c, above2, i_send).start()
+                for c in range(CHUNKS):
+                    send_up(tick, c, above, j_send).start()
 
             pair_up(tick, 1).wait_recv()
             both[...] = times(lowb[tick, 1], mh, ml)
+
+        @pl.when(row < n_rows - 1)
+        def _():
+            for m in (0, 1):
+                send_down(tick, m).start()
 
         @pl.when(tick < ticks - 1)
         def _():
@@ -324,7 +347,12 @@
                         part = pl.ds(c * chunk, chunk)
                         outb[tick, part, :] = outb[tick, part, :] + times(
                             inflow[tick, part, :], nh, nl)
-                        start_up(tick, c)
+                        send_up(tick, c, above2, i_send).start()
+
+                @pl.when(row > 0)
+                def _():
+                    for c in range(CHUNKS):
+                        send_up(tick, c, above, j_send).start()
 
                 lh, ll = split(lowb[tick, 1])
                 correct((lowb[tick, 0] + times(inflow[tick], lh, ll)).T)
@@ -363,7 +391,8 @@
 
         @pl.when(row < n_rows - 1)
         def _():
-            send_down(tick).wait_send()
+            for m in (0, 1):
+                send_down(tick, m).wait_send()
 
     out_copy.wait()
 
@@ -377,16 +406,12 @@
         chips = n_cols // 2
         dma = pltpu.SemaphoreType.DMA
         hops = max(chips - 1, 1)
-        edge, flow = (ticks, block, width), (ticks, width, block)
+        edge, flow = (ticks, 2, block, width), (ticks, width, block)
         return pl.pallas_call(
             functools.partial(kernel, n_rows, n_cols),
             out_shape=jax.ShapeDtypeStruct(vectors.shape, f32),
-            in_specs=[
-                pl.BlockSpec(memory_space=pl.ANY),
-                pl.BlockSpec(memory_space=pl.ANY),
-                pl.BlockSpec(memory_space=pl.ANY),
-                pl.BlockSpec(memory_space=pltpu.SMEM),
-            ],
+            in_specs=[pl.BlockSpec(memory_space=pltpu.HBM)] * 3
+            + [pl.BlockSpec(memory_space=pltpu.SMEM)],
             out_specs=pl.BlockSpec(memory_space=pl.ANY),
             scratch_shapes=[
                 pltpu.VMEM((ticks, per * n_cols, height, block), f32),
@@ -404,10 +429,10 @@
                 dma((ticks,)), dma((ticks,)),
                 dma((ticks, hops, per)), dma((ticks, hops, per)),
                 dma((ticks, CHUNKS)), dma((ticks, CHUNKS)), dma((ticks, CHUNKS)),
-                dma((ticks,)), dma((ticks,)), dma((ticks, 2)), dma((ticks, 2)),
+                dma((ticks, 2)), dma((ticks, 2)), dma((ticks, 2)), dma((ticks, 2)),
             ],
             compiler_params=pltpu.CompilerParams(
-                collective_id=0, has_side_effects=True, vmem_limit_bytes=63 * 2**20),
+                collective_id=0, has_side_effects=True, vmem_limit_bytes=64900000),
         )(vectors, reflectors, factors, starts)
 
     return jax.shard_map(

time: 80.4 us -> 80.3 us (level)
  no operation moved by 1% of the time
where the time goes in v3:
time: 80.3 us; the launch traced here: 79.6 us
  Pallas kernels  77.3 us (96%)
  local copies, waits for them, and re-layouts  2.26 us (3%)
    pallas_call x1, Pallas kernels, on_device(): pl.pallas_call(functools.partial(kernel, n_rows, n_cols), out_shape=jax.S...  77.3 us
    unnamed x1, local copies, waits for them, and re-layouts  2.26 us

profile of v3, /device:TPU:0, one launch (start us, length us, event | category | flops | bytes accessed | tf_op | source)
XLA Modules:
  0.0 79.6 jit_solution(2250510851782942701)
XLA Ops:
  0.0 77.3 %shard_map.46 = f32[2048,128]{1,0:T(8,128)} custom-call(f32[2048,128]{1,0:T(8,128)} %vec_ref.1, f32[3,4,256,128]{3,2,1,0:T(8,128)} %refl_ref.1, f32[3,4,128,128]{3,2,1,0:T(8,128)} %fact_ref.1, s32[3,16]{1,0:T(4,128)} %start_ref.1), custom_call_target="tpu_custom_call" | custom-call | tf_op jit(solution)/shard_map/pallas_call | solution.py:410
  77.3 2.3 %copy.6 = f32[2048,128]{1,0:T(8,128)} copy(f32[2048,128]{1,0:T(8,128)} %shard_map.46) | data formatting | bytes 2097152

commit v4 on v3

--- a/solution.py
+++ b/solution.py
@@ -9,7 +9,7 @@
 
 MESH = pl.DeviceIdType.MESH
 SHIFT = 64
-CHUNKS = 2
+CHUNKS = 4
 f32, bf16 = jnp.float32, jnp.bfloat16
 
 
@@ -38,9 +38,9 @@
 def kernel(
     n_rows, n_cols,
     vec_ref, refl_ref, fact_ref, start_ref, out_ref,
-    gat, fact, work, dense, shifted, inflow, head, outb, tailb, topb, lowb, both,
+    gat, fact, work, dense, shifted, inflow, head, outb, tailb,
     vec_sem, own_sem, fact_sem, g_send, g_recv, p_send, p_recv, f_send, f_recv,
-    i_send, j_send, i_recv, h_send, h_recv, t_send, t_recv,
+    i_send, i_recv, h_send, h_recv,
 ):
     row = lax.axis_index("rows")
     col = lax.axis_index("cols")
@@ -53,9 +53,6 @@
     chip, core = lax.div(col, 2), lax.rem(col, 2)
     partner = chip * 2 + 1 - core
     above, below = lax.rem(row + n_rows - 1, n_rows), lax.rem(row + 1, n_rows)
-    above2, below2 = lax.rem(row + n_rows - 2, n_rows), lax.rem(row + 2, n_rows)
-    upper = lax.rem(row, 2) == 0
-    last_pair = row >= n_rows - 2
 
     def peer_of(j):
         return lax.rem(chip + j, chips) * 2 + core
@@ -80,12 +77,12 @@
     vec_copy.start()
 
     barrier = pltpu.get_barrier_semaphore()
-    for there in (above, below, above2, below2):
+    for there in (above, below):
         pl.semaphore_signal(barrier, inc=1, device_id={"rows": there}, device_id_type=MESH)
     for j in range(1, chips):
         pl.semaphore_signal(barrier, inc=1, device_id={"cols": peer_of(j)}, device_id_type=MESH)
     pl.semaphore_signal(barrier, inc=1, device_id={"cols": partner}, device_id_type=MESH)
-    pl.semaphore_wait(barrier, 4 + chips)
+    pl.semaphore_wait(barrier, 2 + chips)
 
     def to_peer(tick, j, i):
         return pltpu.make_async_remote_copy(
@@ -183,17 +180,11 @@
             work[h, pl.ds(base, reach), :] = (
                 work[h, pl.ds(base, reach), :] - shifted[h, pl.ds(SHIFT - shift, reach), :])
 
-    def send_up(tick, c, there, sems):
+    def send_up(tick, c):
         part = pl.ds(c * chunk, chunk)
         return pltpu.make_async_remote_copy(
             src_ref=outb.at[tick, part], dst_ref=inflow.at[tick, part],
-            send_sem=sems.at[tick, c], recv_sem=i_recv.at[tick, c],
-            device_id={"rows": there}, device_id_type=MESH)
-
-    def pair_up(tick, m):
-        return pltpu.make_async_remote_copy(
-            src_ref=topb.at[tick, m], dst_ref=lowb.at[tick, m],
-            send_sem=t_send.at[tick, m], recv_sem=t_recv.at[tick, m],
+            send_sem=i_send.at[tick, c], recv_sem=i_recv.at[tick, c],
             device_id={"rows": above}, device_id_type=MESH)
 
     def send_down(tick, m):
@@ -268,6 +259,14 @@
                 apply(tick, k)
 
         edge = pl.ds(0, block)
+        outb[tick] = work[0, edge, :].T
+
+        @pl.when(row == n_rows - 1)
+        def _():
+            for c in range(CHUNKS):
+                send_up(tick, c).start()
+            clear_right()
+
         for m in (0, 1):
             tailb[tick, m] = work[m, pl.ds(rows_here, block), :]
 
@@ -285,30 +284,6 @@
                     dot(jnp.concatenate([rh, rl], 1), fcat) + dot(rh, fl))
                 work[1, rows, :] = jnp.zeros((span, block), f32)
 
-        @pl.when(jnp.logical_not(upper))
-        def _():
-            for m in (0, 1):
-                topb[tick, m] = work[m, edge, :].T
-            for m in (0, 1):
-                pair_up(tick, m).start()
-
-        @pl.when(upper)
-        def _():
-            mh, ml = split(work[1, edge, :].T)
-            outb[tick] = work[0, edge, :].T
-            pair_up(tick, 0).wait_recv()
-            outb[tick] = outb[tick] + times(lowb[tick, 0], mh, ml)
-
-            @pl.when(jnp.logical_and(last_pair, row > 0))
-            def _():
-                for c in range(CHUNKS):
-                    send_up(tick, c, above2, i_send).start()
-                for c in range(CHUNKS):
-                    send_up(tick, c, above, j_send).start()
-
-            pair_up(tick, 1).wait_recv()
-            both[...] = times(lowb[tick, 1], mh, ml)
-
         @pl.when(row < n_rows - 1)
         def _():
             for m in (0, 1):
@@ -318,44 +293,20 @@
         def _():
             prepare_own(jnp.minimum(tick + 1, ticks - 1))
 
-        @pl.when(jnp.logical_not(upper))
-        def _():
-            @pl.when(last_pair)
-            def _():
-                clear_right()
-
-            @pl.when(jnp.logical_not(last_pair))
-            def _():
-                for c in range(CHUNKS):
-                    send_up(tick, c, above, j_send).wait_recv()
-                correct(inflow[tick].T)
-
-        @pl.when(upper)
-        def _():
-            @pl.when(last_pair)
-            def _():
-                correct(lowb[tick, 0].T)
-
-            @pl.when(jnp.logical_not(last_pair))
-            def _():
-                nh, nl = split(both[...])
-                for c in range(CHUNKS):
-                    send_up(tick, c, above2, i_send).wait_recv()
-
-                    @pl.when(row > 0)
-                    def _():
-                        part = pl.ds(c * chunk, chunk)
-                        outb[tick, part, :] = outb[tick, part, :] + times(
-                            inflow[tick, part, :], nh, nl)
-                        send_up(tick, c, above2, i_send).start()
+        @pl.when(row < n_rows - 1)
+        def _():
+            mh, ml = split(work[1, edge, :].T)
+            for c in range(CHUNKS):
+                send_up(tick, c).wait_recv()
 
                 @pl.when(row > 0)
                 def _():
-                    for c in range(CHUNKS):
-                        send_up(tick, c, above, j_send).start()
-
-                lh, ll = split(lowb[tick, 1])
-                correct((lowb[tick, 0] + times(inflow[tick], lh, ll)).T)
+                    part = pl.ds(c * chunk, chunk)
+                    outb[tick, part, :] = outb[tick, part, :] + times(
+                        inflow[tick, part, :], mh, ml)
+                    send_up(tick, c).start()
+
+            correct(inflow[tick].T)
 
         @pl.when(tick < ticks - 1)
         def _():
@@ -378,16 +329,10 @@
                 forward(tick, j, i).wait_send()
         to_partner(tick).wait_send()
 
-        @pl.when(jnp.logical_and(upper, row > 0))
+        @pl.when(row > 0)
         def _():
             for c in range(CHUNKS):
-                send_up(tick, c, above2, i_send).wait_send()
-                send_up(tick, c, above, j_send).wait_send()
-
-        @pl.when(jnp.logical_not(upper))
-        def _():
-            for m in (0, 1):
-                pair_up(tick, m).wait_send()
+                send_up(tick, c).wait_send()
 
         @pl.when(row < n_rows - 1)
         def _():
@@ -421,18 +366,15 @@
                 pltpu.VMEM((2, height + 2 * SHIFT, block), f32),
                 pltpu.VMEM(flow, f32), pltpu.VMEM(edge, f32),
                 pltpu.VMEM(flow, f32), pltpu.VMEM(edge, f32),
-                pltpu.VMEM((ticks, 2, block, block), f32),
-                pltpu.VMEM((ticks, 2, block, block), f32),
-                pltpu.VMEM((block, block), f32),
                 dma, dma((ticks,)), dma((ticks,)),
                 dma((ticks, hops, per)), dma((ticks, hops, per)),
                 dma((ticks,)), dma((ticks,)),
                 dma((ticks, hops, per)), dma((ticks, hops, per)),
-                dma((ticks, CHUNKS)), dma((ticks, CHUNKS)), dma((ticks, CHUNKS)),
-                dma((ticks, 2)), dma((ticks, 2)), dma((ticks, 2)), dma((ticks, 2)),
+                dma((ticks, CHUNKS)), dma((ticks, CHUNKS)),
+                dma((ticks, 2)), dma((ticks, 2)),
             ],
             compiler_params=pltpu.CompilerParams(
-                collective_id=0, has_side_effects=True, vmem_limit_bytes=64900000),
+                collective_id=0, has_side_effects=True, vmem_limit_bytes=40 * 2**20),
         )(vectors, reflectors, factors, starts)
 
     return jax.shard_map(

time: 80.3 us -> 79.7 us (level)
  Pallas kernels: 77.3 us -> 74 us
  local copies, waits for them, and re-layouts: 2.26 us -> 5.42 us
    pallas_call x1, Pallas kernels: 77.3 us -> 74 us  [on_device(): pl.pallas_call(functools.partial(kernel, n_rows, n_cols), out_shape=jax.S...]
    unnamed x1 -> x9, local copies, waits for them, and re-layouts: 2.26 us -> 5.42 us
where the time goes in v4:
time: 79.7 us; the launch traced here: 79.5 us
  Pallas kernels  74 us (93%)
  local copies, waits for them, and re-layouts  5.42 us (7%)
    pallas_call x1, Pallas kernels, on_device(): pl.pallas_call(functools.partial(kernel, n_rows, n_cols), out_shape=jax.S...  74 us
    unnamed x9, local copies, waits for them, and re-layouts  5.42 us

profile of v4, /device:TPU:0, one launch (start us, length us, event | category | flops | bytes accessed | tf_op | source)
XLA Modules:
  0.0 79.5 jit_solution(4178142279577470727)
XLA Ops:
  0.0 0.0 copy-start
  0.0 1.4 %copy-done = f32[3,4,256,128]{3,2,1,0:T(8,128)S(1)} copy-done((f32[3,4,256,128]{3,2,1,0:T(8,128)S(1)}, f32[3,4,256,128]{3,2,1,0:T(8,128)}, u32[]{:S(2)}) %copy-start) | copy-done | bytes 1572888
  1.4 0.0 copy-start.1
  1.4 1.2 %copy-done.1 = f32[2048,128]{1,0:T(8,128)S(1)} copy-done((f32[2048,128]{1,0:T(8,128)S(1)}, f32[2048,128]{1,0:T(8,128)}, u32[]{:S(2)}) %copy-start.1) | copy-done | bytes 1048600
  2.6 0.0 copy-start.2
  2.6 1.1 %copy-done.2 = f32[3,4,128,128]{3,2,1,0:T(8,128)S(1)} copy-done((f32[3,4,128,128]{3,2,1,0:T(8,128)S(1)}, f32[3,4,128,128]{3,2,1,0:T(8,128)}, u32[]{:S(2)}) %copy-start.2) | copy-done | bytes 786456
  3.8 0.0 copy-start.3
  3.8 0.7 copy-done.3
  4.5 74.0 %shard_map.46 = f32[2048,128]{1,0:T(8,128)S(1)} custom-call(f32[2048,128]{1,0:T(8,128)S(1)} %copy-done.1, f32[3,4,256,128]{3,2,1,0:T(8,128)S(1)} %copy-done, f32[3,4,128,128]{3,2,1,0:T(8,128)S(1)} %copy-done.2, s32[3,16]{1,0:T(4,128)S(1)} %copy-done.3), custom_call_target="tpu_custom_call" | custom-call | tf_op jit(solution)/shard_map/pallas_call | solution.py:355
  78.5 1.0 %copy.6 = f32[2048,128]{1,0:T(8,128)} copy(f32[2048,128]{1,0:T(8,128)S(1)} %shard_map.46) | data formatting | bytes 2097152
Async XLA Ops:
  0.0 1.4 %copy-start = (f32[3,4,256,128]{3,2,1,0:T(8,128)S(1)}, f32[3,4,256,128]{3,2,1,0:T(8,128)}, u32[]{:S(2)}) copy-start(f32[3,4,256,128]{3,2,1,0:T(8,128)} %refl_ref.1) | copy-start | bytes 4718596
  1.4 1.2 %copy-start.1 = (f32[2048,128]{1,0:T(8,128)S(1)}, f32[2048,128]{1,0:T(8,128)}, u32[]{:S(2)}) copy-start(f32[2048,128]{1,0:T(8,128)} %vec_ref.1) | copy-start | bytes 3145732
  2.6 1.1 %copy-start.2 = (f32[3,4,128,128]{3,2,1,0:T(8,128)S(1)}, f32[3,4,128,128]{3,2,1,0:T(8,128)}, u32[]{:S(2)}) copy-start(f32[3,4,128,128]{3,2,1,0:T(8,128)} %fact_ref.1) | copy-start | bytes 2359300
  3.8 0.7 copy-start.3

commit v5 on v4

--- a/solution.py
+++ b/solution.py
@@ -208,7 +208,10 @@
 
             prepare_share(tick, jnp.where(m == 0, col, partner))
 
-    prepare_own(0)
+    @pl.loop(0, ticks)
+    def _(tick):
+        prepare_own(tick)
+
     vec_copy.wait()
 
     @pl.loop(0, ticks)
@@ -288,10 +291,6 @@
         def _():
             for m in (0, 1):
                 send_down(tick, m).start()
-
-        @pl.when(tick < ticks - 1)
-        def _():
-            prepare_own(jnp.minimum(tick + 1, ticks - 1))
 
         @pl.when(row < n_rows - 1)
         def _():
@@ -374,7 +373,7 @@
                 dma((ticks, 2)), dma((ticks, 2)),
             ],
             compiler_params=pltpu.CompilerParams(
-                collective_id=0, has_side_effects=True, vmem_limit_bytes=40 * 2**20),
+                collective_id=0, has_side_effects=True, vmem_limit_bytes=64900000),
         )(vectors, reflectors, factors, starts)
 
     return jax.shard_map(

time: 79.7 us -> 75.2 us (0.944)
  local copies, waits for them, and re-layouts: 5.42 us -> 2.26 us
  Pallas kernels: 74 us -> 72.7 us
    unnamed x9 -> x1, local copies, waits for them, and re-layouts: 5.42 us -> 2.26 us
    pallas_call x1, Pallas kernels: 74 us -> 72.7 us  [on_device(): pl.pallas_call(functools.partial(kernel, n_rows, n_cols), out_shape=jax.S...]
where the time goes in v5:
time: 75.2 us; the launch traced here: 75 us
  Pallas kernels  72.7 us (97%)
  local copies, waits for them, and re-layouts  2.26 us (3%)
    pallas_call x1, Pallas kernels, on_device(): pl.pallas_call(functools.partial(kernel, n_rows, n_cols), out_shape=jax.S...  72.7 us
    unnamed x1, local copies, waits for them, and re-layouts  2.26 us

profile of v5, /device:TPU:0, one launch (start us, length us, event | category | flops | bytes accessed | tf_op | source)
XLA Modules:
  0.0 75.0 jit_solution(11703882842739469406)
XLA Ops:
  0.0 72.7 %shard_map.46 = f32[2048,128]{1,0:T(8,128)} custom-call(f32[2048,128]{1,0:T(8,128)} %vec_ref.1, f32[3,4,256,128]{3,2,1,0:T(8,128)} %refl_ref.1, f32[3,4,128,128]{3,2,1,0:T(8,128)} %fact_ref.1, s32[3,16]{1,0:T(4,128)} %start_ref.1), custom_call_target="tpu_custom_call" | custom-call | tf_op jit(solution)/shard_map/pallas_call | solution.py:354
  72.7 2.3 %copy.6 = f32[2048,128]{1,0:T(8,128)} copy(f32[2048,128]{1,0:T(8,128)} %shard_map.46) | data formatting | bytes 2097152

commit v6 on v5

--- a/solution.py
+++ b/solution.py
@@ -38,7 +38,7 @@
 def kernel(
     n_rows, n_cols,
     vec_ref, refl_ref, fact_ref, start_ref, out_ref,
-    gat, fact, work, dense, shifted, inflow, head, outb, tailb,
+    gat, fact, flowh, flowl, work, dense, shifted, inflow, head, outb, tailb,
     vec_sem, own_sem, fact_sem, g_send, g_recv, p_send, p_recv, f_send, f_recv,
     i_send, i_recv, h_send, h_recv,
 ):
@@ -140,6 +140,8 @@
     clear_right()
     reset()
     shifted[...] = jnp.zeros_like(shifted)
+    flowh[...] = jnp.zeros_like(flowh)
+    flowl[...] = jnp.zeros_like(flowl)
 
     def in_block(tick, k):
         return jnp.clip(start_ref[tick, k] - row * rows_here - k * block, 0, SHIFT)
@@ -238,27 +240,44 @@
             fetch(n_dia - 1)
             prepare(tick, n_dia - 1)
 
+        def blend(k):
+            rows = pl.ds(pl.multiple_of(k * block, block), block)
+            rh, rl = split(work[1, rows, :])
+            return rows, work[0, rows, :] + (
+                dot(jnp.concatenate([rh, rl], 1), flowh[...]) + dot(rh, flowl[...]))
+
+        def settle(rows, value):
+            work[0, rows, :] = value
+            work[1, rows, :] = zero
+
+        settle(*blend(n_dia - 1))
+
         @pl.loop(0, n_dia)
         def _(counter):
             k = n_dia - 1 - counter
             later = jnp.maximum(k - 1, 0)
-            ahead = jnp.logical_and(k > 0, turns(later) > 0)
-
-            @pl.when(ahead)
+            remote = turns(later) > 0
+
+            @pl.when(jnp.logical_and(k > 0, remote))
             def _():
                 fetch(later)
-
-            @pl.when(jnp.logical_and(k == 0, jnp.logical_and(row > 0, tick > 0)))
-            def _():
-                take_head(jnp.maximum(tick - 1, 0))
-
-            @pl.when(ahead)
-            def _():
+                rows, value = blend(later)
                 apply(tick, k)
                 prepare(tick, later)
-
-            @pl.when(jnp.logical_not(ahead))
-            def _():
+                settle(rows, value)
+
+            @pl.when(jnp.logical_and(k > 0, jnp.logical_not(remote)))
+            def _():
+                rows, value = blend(later)
+                apply(tick, k)
+                settle(rows, value)
+
+            @pl.when(k == 0)
+            def _():
+                @pl.when(jnp.logical_and(row > 0, tick > 0))
+                def _():
+                    take_head(jnp.maximum(tick - 1, 0))
+
                 apply(tick, k)
 
         edge = pl.ds(0, block)
@@ -268,15 +287,12 @@
         def _():
             for c in range(CHUNKS):
                 send_up(tick, c).start()
-            clear_right()
 
         for m in (0, 1):
             tailb[tick, m] = work[m, pl.ds(rows_here, block), :]
 
-        def correct(flow):
-            fh, fl = split(flow)
-            fcat = jnp.concatenate([fh, fh], 0)
-
+        def correct():
+            fcat, fl = flowh[...], flowl[...]
             span = 4 * block
 
             @pl.loop(0, rows_here // span)
@@ -285,7 +301,6 @@
                 rh, rl = split(work[1, rows, :])
                 work[0, rows, :] = work[0, rows, :] + (
                     dot(jnp.concatenate([rh, rl], 1), fcat) + dot(rh, fl))
-                work[1, rows, :] = jnp.zeros((span, block), f32)
 
         @pl.when(row < n_rows - 1)
         def _():
@@ -305,7 +320,14 @@
                         inflow[tick, part, :], mh, ml)
                     send_up(tick, c).start()
 
-            correct(inflow[tick].T)
+            fh, fl = split(inflow[tick].T)
+            flowh[pl.ds(0, block), :] = fh
+            flowh[pl.ds(block, block), :] = fh
+            flowl[...] = fl
+
+            @pl.when(tick == ticks - 1)
+            def _():
+                correct()
 
         @pl.when(tick < ticks - 1)
         def _():
@@ -360,6 +382,7 @@
             scratch_shapes=[
                 pltpu.VMEM((ticks, per * n_cols, height, block), f32),
                 pltpu.VMEM((ticks, per, block, block), f32),
+                pltpu.VMEM((2 * block, width), bf16), pltpu.VMEM((block, width), bf16),
                 pltpu.VMEM((2, rows_here + height - block + SHIFT, block), f32),
                 pltpu.VMEM((ticks * per * n_cols, 2 * height, height), bf16),
                 pltpu.VMEM((2, height + 2 * SHIFT, block), f32),

time: 75.2 us -> 75 us (level)
  no operation moved by 1% of the time
where the time goes in v6:
time: 75 us; the launch traced here: 74.8 us
  Pallas kernels  72.5 us (97%)
  local copies, waits for them, and re-layouts  2.26 us (3%)
    pallas_call x1, Pallas kernels, on_device(): pl.pallas_call(functools.partial(kernel, n_rows, n_cols), out_shape=jax.S...  72.5 us
    unnamed x1, local copies, waits for them, and re-layouts  2.26 us

profile of v6, /device:TPU:0, one launch (start us, length us, event | category | flops | bytes accessed | tf_op | source)
XLA Modules:
  0.0 74.8 jit_solution(12653643181914741714)
XLA Ops:
  0.0 72.5 %shard_map.46 = f32[2048,128]{1,0:T(8,128)} custom-call(f32[2048,128]{1,0:T(8,128)} %vec_ref.1, f32[3,4,256,128]{3,2,1,0:T(8,128)} %refl_ref.1, f32[3,4,128,128]{3,2,1,0:T(8,128)} %fact_ref.1, s32[3,16]{1,0:T(4,128)} %start_ref.1), custom_call_target="tpu_custom_call" | custom-call | tf_op jit(solution)/shard_map/pallas_call | solution.py:376
  72.5 2.3 %copy.6 = f32[2048,128]{1,0:T(8,128)} copy(f32[2048,128]{1,0:T(8,128)} %shard_map.46) | data formatting | bytes 2097152
